TPU v7x, 32 devices: a whole 2x2x4 slice. The times are simulated.
32 devices in a mesh: patch: 2 (over y), exp: 4 (over z), tile: 2 (over x), band: 2 (over core).
Axes of the slice: x: 2, y: 2, z: 4, core: 2. Of those that a mesh axis runs over, the one named last changes fastest.
Arguments:
- images: bfloat16 [4, 2, 64, 128, 128], P(('patch', 'band'), 'tile', 'exp'), parts along dimension 0, may hold values from -6 to 6
- mask_bits: int32 [4, 2, 64, 128, 128], P(('patch', 'band'), 'tile', 'exp'), parts along dimension 0, may hold values from 0 to 7
- inv_var: float32 [4, 2, 64], P(('patch', 'band'), 'tile', 'exp'), parts along dimension 0, may hold values from 0.5 to 4
- routes: int32 [4, 2, 64, 1], P(('patch', 'band'), 'tile', 'exp'), parts along dimension 0, may hold values from 0 to 3; in each aligned block of 16 rows (0 to 15, 16 to 31, ..., all dimensions but the last counted through in order) at most 8 rows name the same one
- block_slot: int32 [4, 2, 64], P(('patch', 'band'), 'tile', 'exp'), parts along dimension 0, may hold values from 0 to 7
- kernel_index: int32 [4, 2, 64], P(('patch', 'band'), 'tile', 'exp'), parts along dimension 0, may hold values from 0 to 63
- coefficients: float32 [64, 3], replicated, may hold values from -4 to 4
Outputs:
- coadd: float32 [4, 512, 2048], P(('patch', 'band'), 'tile', 'exp'), parts along dimension 0
- detection: float32 [1024, 2048], P(('patch', 'tile'), 'exp'), parts along dimension 0
There are 2 independent parts, one for each index of `patch`. A program takes and returns all parts, laid end to end along the dimension named above; an argument that names none is the same for every part. Nothing has to cross between parts.
Inputs may be any that keep to these rules, and one draw needn't show every extreme that they name: Among the 16 sub-blocks of one device for one band and strip (an aligned block of routes), no tile column is named more than 8 times, and some tile column is named exactly 8 times.
All inputs are finite; a program needn't handle non-finite values.
Results may differ from a plain program's by a relative error of at most 0.0039.
Values may be sent and summed in bfloat16 or wider, within the bound.
A program may use at most 128 MiB of HBM per device.

v0:
```python
import functools

import jax
import jax.numpy as jnp
import numpy as np
from jax import lax
from jax.experimental import pallas as pl
from jax.experimental.pallas import tpu as pltpu
from jax.sharding import PartitionSpec as P

BLOCK = 128
TAPS = 41
BLOCK_ROWS = 2
BLOCK_COLS = 4
SPILL = 24

kernel_sigmas = (1.0, 2.5, 6.0)
MESH = pl.DeviceIdType.MESH


def tap_matrix(rows, cols, shift):
    half_span = TAPS // 2
    offset = np.arange(rows)[:, None] - np.arange(cols)[None, :] - shift
    axis = np.arange(-half_span, half_span + 1).astype(np.float64)
    result = []
    for spread in kernel_sigmas:
        norm = np.sum(np.exp(-axis * axis / (2.0 * spread * spread)))
        result.append(
            np.where(
                np.abs(offset) <= half_span,
                np.exp(-offset * offset / (2.0 * spread * spread)),
                0.0,
            )
            / norm
        )
    return np.stack(result)


def tap_pair(taps):
    high = taps.astype(jnp.bfloat16)
    low = (taps - high.astype(np.float64)).astype(jnp.bfloat16)
    return jnp.asarray(np.stack([high, low]))


def split(value):
    high = value.astype(jnp.bfloat16)
    return high, (value - high.astype(jnp.float32)).astype(jnp.bfloat16)


def products(pairs):
    total = None
    for left, right in pairs:
        term = jnp.dot(left, right, preferred_element_type=jnp.float32)
        total = term if total is None else total + term
    return total


def place_kernel(
    held, routes, slots, kernels, inverse, coefs, images, masks, depth, basis, acc
):
    d = pl.program_id(0)
    acc[...] = jnp.zeros_like(acc)

    def one(i, carry):
        @pl.when(routes[i] == d)
        def _():
            slot = slots[i]
            which = kernels[i]
            rows = pl.ds(pl.multiple_of(slot // BLOCK_COLS * BLOCK, BLOCK), BLOCK)
            cols = pl.ds(pl.multiple_of(slot % BLOCK_COLS * BLOCK, BLOCK), BLOCK)
            bits = masks[i]
            suspect = jnp.bitwise_and(bits, 1).astype(jnp.float32)
            usable = jnp.where(jnp.bitwise_and(bits, 6) == 6, 0.0, 1.0 - 0.5 * suspect)
            scaled = usable * inverse[i]
            weighted = (
                (scaled * images[i].astype(jnp.float32)).astype(jnp.bfloat16).astype(jnp.float32)
            )
            weight = scaled.astype(jnp.bfloat16).astype(jnp.float32)
            for k in range(3):
                acc[k, rows, cols] += coefs[k, which] * weighted
            acc[3, rows, cols] += weight

        return carry

    lax.fori_loop(0, held, one, 0)
    depth[0] = acc[3].astype(jnp.bfloat16)
    basis[0, 0], basis[0, 1] = split(acc[0])
    basis[0, 2] = acc[1].astype(jnp.bfloat16)
    basis[0, 3] = acc[2].astype(jnp.bfloat16)


def reduce_kernel(
    n, strips, bands, depth, basis, across, down, numerator, denominator, det_mine, det_theirs,
    moving, outgoing, incoming, framed, result, spilling, spilled,
    send_sem, recv_sem, match_send, match_recv,
    spill_send, spill_recv, det_send, det_recv, frame_sem,
):
    me = lax.axis_index("exp")
    strip = lax.axis_index("tile")
    band = lax.axis_index("band")
    rows_all = depth.shape[1]
    chunk = 32
    barrier = pltpu.get_barrier_semaphore()
    greet = [
        (strip > 0, {"tile": strip - 1}),
        (strip < strips - 1, {"tile": strip + 1}),
    ]
    for here, peer in greet:

        @pl.when(here)
        def _(peer=peer):
            pl.semaphore_signal(barrier, inc=1, device_id=peer, device_id_type=MESH)

    for j in range(1, n):
        pl.semaphore_signal(
            barrier, inc=1, device_id={"exp": lax.rem(me + j, n)}, device_id_type=MESH
        )
    for j in range(1, bands):
        pl.semaphore_signal(
            barrier, inc=1, device_id={"band": lax.rem(band + j, bands)}, device_id_type=MESH
        )
    peers = bands - 1 + n - 1
    for here, _peer in greet:
        peers = peers + here.astype(jnp.int32)
    pl.semaphore_wait(barrier, peers)

    tile_cols = depth.shape[2]
    half = tile_cols // 2

    def frame_copies(j, slot):
        d = lax.rem(me + j, n)
        before = jnp.maximum(d - 1, 0)
        after = jnp.minimum(d + 1, n - 1)
        whole = pl.ds(BLOCK, tile_cols)
        return (
            pltpu.make_async_copy(
                basis.at[d], framed.at[slot, :, :, whole], frame_sem.at[slot, 0]
            ),
            pltpu.make_async_copy(
                basis.at[before, :, :, pl.ds(tile_cols - BLOCK, BLOCK)],
                framed.at[slot, :, :, pl.ds(0, BLOCK)],
                frame_sem.at[slot, 1],
            ),
            pltpu.make_async_copy(
                basis.at[after, :, :, pl.ds(0, BLOCK)],
                framed.at[slot, :, :, pl.ds(BLOCK + tile_cols, BLOCK)],
                frame_sem.at[slot, 2],
            ),
        )

    def spill_copy(side, j):
        peer = strip + 1 if side == 0 else strip - 1
        return pltpu.make_async_remote_copy(
            src_ref=spilling.at[side, j],
            dst_ref=spilled.at[side, j],
            send_sem=spill_send.at[side, j],
            recv_sem=spill_recv.at[side, j],
            device_id={"tile": peer},
            device_id_type=MESH,
        )

    sends_spill = (strip < strips - 1, strip > 0)
    gets_spill = (strip > 0, strip < strips - 1)
    for side in range(2):

        @pl.when(jnp.logical_not(gets_spill[side]))
        def _(side=side):
            spilled[side] = jnp.zeros(spilled.shape[1:], spilled.dtype)

    def correlate(j, slot):
        d = lax.rem(me + j, n)
        for copy in frame_copies(j, slot):
            copy.wait()

        @pl.when(d == 0)
        def _():
            framed[slot, :, :, 0:BLOCK] = jnp.zeros(
                framed.shape[1:3] + (BLOCK,), framed.dtype
            )

        @pl.when(d == n - 1)
        def _():
            framed[slot, :, :, BLOCK + tile_cols :] = jnp.zeros(
                framed.shape[1:3] + (BLOCK,), framed.dtype
            )

        first = (framed[slot, 0], framed[slot, 1])
        tall_high, tall_low = split(
            products(((down[0, 0], first[0]), (down[0, 0], first[1]), (down[1, 0], first[0])))
        )
        second = framed[slot, 2]
        tall_second = products(((down[0, 1], second), (down[1, 1], second))).astype(jnp.bfloat16)
        tall_third = products(((down[0, 2], framed[slot, 3]),)).astype(jnp.bfloat16)
        for h in range(2):
            cols = slice(h * half, h * half + half + 2 * BLOCK)
            total = products((
                (tall_high[:, cols], across[0, 0]),
                (tall_high[:, cols], across[1, 0]),
                (tall_low[:, cols], across[0, 0]),
                (tall_second[:, cols], across[0, 1]),
                (tall_second[:, cols], across[1, 1]),
                (tall_third[:, cols], across[0, 2]),
            ))
            out = slice(h * half, (h + 1) * half)
            result[slot, :, out] = total[SPILL : SPILL + rows_all]
            spilling[0, j, :, out] = total[SPILL + rows_all :].astype(jnp.bfloat16)
            spilling[1, j, :, out] = total[0:SPILL].astype(jnp.bfloat16)
        for side in range(2):

            @pl.when(sends_spill[side])
            def _(side=side):
                spill_copy(side, j).start()

    def unit_copy(d, right):
        place = d if right else jnp.where(d == me - 1, n, d)
        return pltpu.make_async_remote_copy(
            src_ref=moving.at[d],
            dst_ref=moving.at[place],
            send_sem=send_sem.at[d],
            recv_sem=recv_sem.at[place],
            device_id={"exp": me + 1 if right else me - 1},
            device_id_type=MESH,
        )

    def arrived(place):
        pltpu.make_async_remote_copy(
            src_ref=moving.at[place],
            dst_ref=moving.at[place],
            send_sem=send_sem.at[0],
            recv_sem=recv_sem.at[place],
            device_id={"band": lax.rem(band + 1, bands)},
            device_id_type=MESH,
        ).wait_recv()

    def pass_on(d, right, gets):
        @pl.when(gets)
        def _():
            arrived(d)
            for r in range(0, rows_all, chunk):
                rows = slice(r, r + chunk)
                moving[d, rows] = (
                    moving[d, rows].astype(jnp.float32) + depth[d, rows].astype(jnp.float32)
                ).astype(jnp.bfloat16)

        @pl.when(jnp.logical_not(gets))
        def _():
            for r in range(0, rows_all, chunk):
                moving[d, r : r + chunk] = depth[d, r : r + chunk]

        unit_copy(d, right).start()

    def match_copy(j):
        return pltpu.make_async_remote_copy(
            src_ref=outgoing.at[j],
            dst_ref=incoming.at[j],
            send_sem=match_send.at[j],
            recv_sem=match_recv.at[j],
            device_id={"exp": lax.rem(me + j, n)},
            device_id_type=MESH,
        )

    def complete(j, slot):
        for side in range(2):

            @pl.when(gets_spill[side])
            def _(side=side):
                spill_copy(side, j).wait_recv()

        low = rows_all - SPILL
        result[slot, 0:SPILL] += spilled[0, j].astype(jnp.float32)
        result[slot, low:] += spilled[1, j].astype(jnp.float32)
        if isinstance(j, int):
            numerator[...] = result[slot]
        else:
            for r in range(0, rows_all, chunk):
                outgoing[j, r : r + chunk] = result[slot, r : r + chunk].astype(jnp.bfloat16)

    def step_right(s, carry):
        @pl.when(n - 1 - s > me)
        def _():
            pass_on(n - 1 - s, True, me > 0)

        return carry

    def step_left(s, carry):
        @pl.when(s < me)
        def _():
            pass_on(s, False, me < n - 1)

        return carry

    right_first = 2 * me < n - 1
    left_first = jnp.logical_not(right_first)

    def pick(i):
        down_from = n - 1 - i
        right = jnp.where(down_from > me, down_from, down_from - 1)
        left = jnp.where(i < me, i, i + 1)
        d = jnp.where(right_first, right, left)
        return jnp.where(i == n - 1, 0, lax.rem(d - me + n, n))

    for copy in frame_copies(pick(0), 0):
        copy.start()

    @pl.when(me == 0)
    def _():
        lax.fori_loop(0, n - 1, step_right, 0)

    @pl.when(me == n - 1)
    def _():
        lax.fori_loop(0, n - 1, step_left, 0)

    def turn(i, carry):
        j = pick(i)
        slot = lax.rem(i, 2)

        @pl.when(i < n - 1)
        def _():
            for copy in frame_copies(pick(i + 1), 1 - slot):
                copy.start()

        correlate(j, slot)

        @pl.when(i > 0)
        def _():
            earlier = pick(i - 1)
            complete(earlier, 1 - slot)
            match_copy(earlier).start()

        @pl.when((i > 0) & right_first & (me > 0))
        def _():
            step_right(i - 1, 0)

        @pl.when((i > 0) & left_first & (me < n - 1))
        def _():
            step_left(i - 1, 0)

        return carry

    lax.fori_loop(0, n, turn, 0)
    complete(0, (n - 1) % 2)

    @pl.when(right_first)
    def _():
        @pl.when(me > 0)
        def _():
            lax.fori_loop(n - 1, n - 1, step_right, 0)

        lax.fori_loop(0, n - 1, step_left, 0)

    @pl.when(left_first)
    def _():
        @pl.when(me < n - 1)
        def _():
            lax.fori_loop(n - 1, n - 1, step_left, 0)

        lax.fori_loop(0, n - 1, step_right, 0)

    @pl.when(me > 0)
    def _():
        arrived(me)

    @pl.when(me == 0)
    def _():
        moving[me] = jnp.zeros(moving.shape[1:], moving.dtype)

    @pl.when(me < n - 1)
    def _():
        arrived(n)

    @pl.when(me == n - 1)
    def _():
        moving[n] = jnp.zeros(moving.shape[1:], moving.dtype)

    def gather(i, carry):
        j = i + 1
        match_copy(j).wait_recv()
        for r in range(0, rows_all, chunk):
            rows = slice(r, r + chunk)
            numerator[rows] += incoming[j, rows].astype(jnp.float32)
        return carry

    lax.fori_loop(0, n - 1, gather, 0)
    def det_copy(j, h):
        rows = pl.ds(h * rows_all // 2, rows_all // 2)
        return pltpu.make_async_remote_copy(
            src_ref=det_mine.at[rows],
            dst_ref=det_theirs.at[j - 1, rows],
            send_sem=det_send.at[j - 1, h],
            recv_sem=det_recv.at[j - 1, h],
            device_id={"band": lax.rem(band + j, bands)},
            device_id_type=MESH,
        )

    for h in range(2):
        for r in range(h * rows_all // 2, (h + 1) * rows_all // 2, chunk):
            rows = slice(r, r + chunk)
            below = 1.0 + (
                depth[me, rows].astype(jnp.float32)
                + moving[me, rows].astype(jnp.float32)
                + moving[n, rows].astype(jnp.float32)
            )
            denominator[rows] = below
            value = numerator[rows] / below
            det_mine[rows] = value * value * below
        for j in range(1, bands):
            det_copy(j, h).start()
    for h in range(2):
        for j in range(1, bands):
            det_copy(j, h).wait()

    def drain(s, carry):
        to_right = n - 1 - s
        match_copy(s + 1).wait_send()

        @pl.when(to_right > me)
        def _():
            unit_copy(to_right, True).wait_send()

        @pl.when(s < me)
        def _():
            unit_copy(s, False).wait_send()

        return carry

    lax.fori_loop(0, n - 1, drain, 0)

    def drain_spill(j, carry):
        for side in range(2):

            @pl.when(sends_spill[side])
            def _(side=side):
                spill_copy(side, j).wait_send()

        return carry

    lax.fori_loop(0, n, drain_spill, 0)


def finish_kernel(numerator, denominator, det_mine, det_theirs, coadd, detection):
    coadd[...] = numerator[...] / denominator[...]
    value = det_mine[...]
    for j in range(det_theirs.shape[0]):
        value += det_theirs[j]
    detection[...] = value


def local(sizes, images, mask_bits, inv_var, routes, block_slot, kernel_index, coefficients):
    n, strips, bands = sizes["exp"], sizes["tile"], sizes["band"]
    held = images.shape[2]
    tile_rows = BLOCK_ROWS * BLOCK
    tile_cols = BLOCK_COLS * BLOCK
    half = tile_cols // 2
    across = tap_pair(tap_matrix(2 * half, half, BLOCK))
    down = tap_pair(tap_matrix(tile_rows + 2 * SPILL, tile_rows, SPILL))
    smem = pl.BlockSpec(memory_space=pltpu.SMEM)
    vmem = pl.BlockSpec(memory_space=pltpu.VMEM)
    depth, basis = pl.pallas_call(
        functools.partial(place_kernel, held),
        grid=(n,),
        out_shape=(
            jax.ShapeDtypeStruct((n, tile_rows, tile_cols), jnp.bfloat16),
            jax.ShapeDtypeStruct((n, 4, tile_rows, tile_cols), jnp.bfloat16),
        ),
        in_specs=[smem] * 5 + [vmem] * 2,
        out_specs=(
            pl.BlockSpec((1, tile_rows, tile_cols), lambda d: (d, 0, 0)),
            pl.BlockSpec((1, 4, tile_rows, tile_cols), lambda d: (d, 0, 0, 0)),
        ),
        scratch_shapes=[pltpu.VMEM((4, tile_rows, tile_cols), jnp.float32)],
        name="place",
    )(
        routes[0, 0, :, 0], block_slot[0, 0], kernel_index[0, 0], inv_var[0, 0],
        coefficients.T, images[0, 0], mask_bits[0, 0],
    )
    whole = jax.ShapeDtypeStruct((tile_rows, tile_cols), jnp.float32)
    others = jax.ShapeDtypeStruct((bands - 1, tile_rows, tile_cols), jnp.float32)
    numerator, denominator, det_mine, det_theirs = pl.pallas_call(
        functools.partial(reduce_kernel, n, strips, bands),
        out_shape=(whole, whole, whole, others),
        in_specs=[vmem, pl.BlockSpec(memory_space=pl.ANY), vmem, vmem],
        out_specs=(vmem,) * 4,
        scratch_shapes=[
            pltpu.VMEM((n + 1, tile_rows, tile_cols), jnp.bfloat16),
            pltpu.VMEM((n, tile_rows, tile_cols), jnp.bfloat16),
            pltpu.VMEM((n, tile_rows, tile_cols), jnp.bfloat16),
            pltpu.VMEM((2, 4, tile_rows, tile_cols + 2 * BLOCK), jnp.bfloat16),
            pltpu.VMEM((2, tile_rows, tile_cols), jnp.float32),
            pltpu.VMEM((2, n, SPILL, tile_cols), jnp.bfloat16),
            pltpu.VMEM((2, n, SPILL, tile_cols), jnp.bfloat16),
            pltpu.SemaphoreType.DMA((n,)),
            pltpu.SemaphoreType.DMA((n + 1,)),
            pltpu.SemaphoreType.DMA((n,)),
            pltpu.SemaphoreType.DMA((n,)),
            pltpu.SemaphoreType.DMA((2, n)),
            pltpu.SemaphoreType.DMA((2, n)),
            pltpu.SemaphoreType.DMA((bands - 1, 2)),
            pltpu.SemaphoreType.DMA((bands - 1, 2)),
            pltpu.SemaphoreType.DMA((2, 3)),
        ],
        compiler_params=pltpu.CompilerParams(collective_id=0, has_side_effects=True),
        name="correlate_and_reduce",
    )(depth, basis, across, down)
    part = pl.BlockSpec((tile_rows // 4, tile_cols), lambda i: (i, 0))
    coadd, detection = pl.pallas_call(
        finish_kernel,
        grid=(4,),
        out_shape=(whole, whole),
        in_specs=[part] * 3
        + [pl.BlockSpec((bands - 1, tile_rows // 4, tile_cols), lambda i: (0, i, 0))],
        out_specs=(part, part),
        name="finish",
    )(numerator, denominator, det_mine, det_theirs)
    return coadd[None], detection


def solution(mesh):
    return jax.shard_map(
        functools.partial(local, dict(mesh.shape)),
        mesh=mesh,
        in_specs=(
            P(("patch", "band"), "tile", "exp", None, None),
            P(("patch", "band"), "tile", "exp", None, None),
            P(("patch", "band"), "tile", "exp"),
            P(("patch", "band"), "tile", "exp", None),
            P(("patch", "band"), "tile", "exp"),
            P(("patch", "band"), "tile", "exp"),
            P(),
        ),
        out_specs=(P(("patch", "band"), "tile", "exp"), P(("patch", "tile"), "exp")),
        check_vma=False,
    )
```

profile of v0, /device:TPU:9, one launch (start us, length us, event | category | flops | bytes accessed | tf_op | source)
XLA Modules:
  0.0 59.2 jit_solution(3649087661309358974)
XLA Ops:
  0.6 5.6 %place.1 = (bf16[4,256,512]{2,1,0:T(8,128)(2,1)}, bf16[4,4,256,512]{3,2,1,0:T(8,128)(2,1)}) custom-call(s32[16]{0:T(128)} %bitcast.11, s32[16]{0:T(128)} %bitcast.12, s32[16]{0:T(128)} %bitcast.13, f32[16]{0:T(128)} %bitcast.14, f32[3,64]{1,0:T(4,128)} %bitcast.10, bf16[16,128,128]{2,1,0:T(8,128)(2,1)} %bitcast.9, s32[16,128,128]{2,1,0:T(8,128)} %bitcast.8), custom_call_target="tpu_custom_call" | custom-call | tf_op jit(solution)/shard_map/place/pallas_call | solution.py:458
  6.3 49.3 %correlate_and_reduce.1 = (f32[256,512]{1,0:T(8,128)}, f32[256,512]{1,0:T(8,128)}, f32[256,512]{1,0:T(8,128)}, f32[1,256,512]{2,1,0:T(8,128)}) custom-call(bf16[4,256,512]{2,1,0:T(8,128)(2,1)} %get-tuple-element.10.depth, bf16[4,4,256,512]{3,2,1,0:T(8,128)(2,1)} %get-tuple-element.11.basis, bf16[2,3,512,256]{3,2,1,0:T(8,128)(2,1)} %constant.4.clone.across, ...), custom_call_target="tpu_custom_call" | custom-call | tf_op jit(solution)/shard_map/correlate_and_reduce/pallas_call | solution.py:478
  55.6 3.6 %finish.1 = (f32[256,512]{1,0:T(8,128)}, f32[256,512]{1,0:T(8,128)}) custom-call(f32[256,512]{1,0:T(8,128)} %get-tuple-element.12.numerator, f32[256,512]{1,0:T(8,128)} %get-tuple-element.13.denominator, f32[256,512]{1,0:T(8,128)} %get-tuple-element.14.det_mine, f32[1,256,512]{2,1,0:T(8,128)} %get-tuple-element.15.det_theirs), custom_call_target="tpu_custom_call" | custom-call | tf_op jit(solution)/shard_map/finish/pallas_call | solution.py:505
where the time goes:
time: 59.5 us; the launch traced here: 59.2 us
  Pallas kernels  58.6 us (98%)
  between operations  0.64 us (1%)
    pallas_call x1, Pallas kernels, local(): pl.pallas_call(functools.partial(reduce_kernel, n, strips, bands), out_sh...  49.3 us
    pallas_call x1, Pallas kernels, local(): pl.pallas_call(functools.partial(place_kernel, held), grid=(n,), out_shap...  5.63 us
    pallas_call x1, Pallas kernels, local(): pl.pallas_call(finish_kernel, grid=(4,), out_shape=(whole, whole), in_spe...  3.62 us

commit v1 on v0

v1 whole, which is shorter than its diff:
```python
import functools

import jax
import jax.numpy as jnp
import numpy as np
from jax import lax
from jax.experimental import pallas as pl
from jax.experimental.pallas import tpu as pltpu
from jax.sharding import PartitionSpec as P

TAPS = 41
BLOCK_ROWS = 2
BLOCK_COLS = 4
SLOTS = BLOCK_ROWS * BLOCK_COLS
SPILL = 24
CHUNKS = 4
PARTS = 4

kernel_sigmas = (1.0, 2.5, 6.0)
MESH = pl.DeviceIdType.MESH


def tap_matrix(rows, cols, shift):
    half_span = TAPS // 2
    offset = np.arange(rows)[:, None] - np.arange(cols)[None, :] - shift
    axis = np.arange(-half_span, half_span + 1).astype(np.float64)
    result = []
    for spread in kernel_sigmas:
        norm = np.sum(np.exp(-axis * axis / (2.0 * spread * spread)))
        result.append(
            np.where(
                np.abs(offset) <= half_span,
                np.exp(-offset * offset / (2.0 * spread * spread)),
                0.0,
            )
            / norm
        )
    return np.stack(result)


def tap_pair(taps):
    high = taps.astype(jnp.bfloat16)
    low = (taps - high.astype(np.float64)).astype(jnp.bfloat16)
    return jnp.asarray(np.stack([high, low]))


def split(value):
    high = value.astype(jnp.bfloat16)
    return high, (value - high.astype(jnp.float32)).astype(jnp.bfloat16)


def products(pairs):
    total = None
    for left, right in pairs:
        term = jnp.dot(left, right, preferred_element_type=jnp.float32)
        total = term if total is None else total + term
    return total


def coadd_kernel(
    n, strips, bands,
    routes, slots, kernels, inverse, coefs, images, masks, across, down,
    coadd, detection,
    pictures, bits_in, weights, raw, acc, planes, own_depth, raw_depth, table, raw_table,
    frame, result, depth_moving, moving, last_out, last_in, spilling, spilled,
    below, det_mine, det_theirs,
    in_sem, raw_send, raw_recv, table_sem, depth_send, depth_recv, send_sem, recv_sem,
    last_send, last_recv, spill_send, spill_recv, det_send, det_recv,
):
    me = lax.axis_index("exp")
    strip = lax.axis_index("tile")
    band = lax.axis_index("band")
    held, block = pictures.shape[0], pictures.shape[1]
    span = block // CHUNKS
    rows_all, tile_cols = result.shape[1:]
    part = rows_all // PARTS
    half = tile_cols // 2
    at_left, at_right = me == 0, me == n - 1
    at_end = at_left | at_right
    gets_raw_left, gets_raw_right = me == 1, me == n - 2
    left_half = 2 * me < n - 1

    def input_copies(c):
        rows = pl.ds(pl.multiple_of(c * span, span), span)
        return (
            pltpu.make_async_copy(masks.at[:, rows], bits_in.at[:, rows], in_sem.at[c, 0]),
            pltpu.make_async_copy(images.at[:, rows], pictures.at[:, rows], in_sem.at[c, 1]),
        )

    for c in range(CHUNKS):
        for copy in input_copies(c):
            copy.start()

    barrier = pltpu.get_barrier_semaphore()
    greet = [
        (strip > 0, {"tile": strip - 1}),
        (strip < strips - 1, {"tile": strip + 1}),
        (me > 0, {"exp": me - 1}),
        (me < n - 1, {"exp": me + 1}),
    ]
    peers = bands - 1
    for here, peer in greet:

        @pl.when(here)
        def _(peer=peer):
            pl.semaphore_signal(barrier, inc=1, device_id=peer, device_id_type=MESH)

        peers = peers + here.astype(jnp.int32)
    for j in range(1, bands):
        pl.semaphore_signal(
            barrier, inc=1, device_id={"band": lax.rem(band + j, bands)}, device_id_type=MESH
        )

    keys = [routes[i] * SLOTS + slots[i] for i in range(held)]
    for i in range(held):
        before = held
        for j in range(i):
            before = jnp.where(keys[j] == keys[i], j, before)
        table[i] = jnp.int32(before)

    def note_last(key, carry):
        last = held
        for i in range(held):
            last = jnp.where(routes[i] * SLOTS + slots[i] == key - SLOTS, i, last)
        table[held + key] = last
        return carry

    lax.fori_loop(0, (n + 2) * SLOTS, note_last, 0)

    def last_of(entries, d, slot):
        return entries[held + (d + 1) * SLOTS + slot]

    none = jnp.zeros((block, block), jnp.float32)
    for k in range(3):
        acc[held, k] = none
    for k in range(4):
        planes[held, k] = none.astype(jnp.bfloat16)
    own_depth[held] = none
    raw_depth[held] = none

    sends_spill = (strip < strips - 1, strip > 0)
    gets_spill = (strip > 0, strip < strips - 1)
    for side in range(2):

        @pl.when(jnp.logical_not(gets_spill[side]))
        def _(side=side):
            spilled[side] = jnp.zeros(spilled.shape[1:], spilled.dtype)

    pl.semaphore_wait(barrier, peers)

    inward = jnp.where(at_left, 1, n - 2)

    def raw_copy(c):
        return pltpu.make_async_remote_copy(
            src_ref=weights.at[c],
            dst_ref=raw.at[c],
            send_sem=raw_send.at[c],
            recv_sem=raw_recv.at[c],
            device_id={"exp": inward},
            device_id_type=MESH,
        )

    def table_copy():
        return pltpu.make_async_remote_copy(
            src_ref=table,
            dst_ref=raw_table,
            send_sem=table_sem.at[0],
            recv_sem=table_sem.at[1],
            device_id={"exp": inward},
            device_id_type=MESH,
        )

    @pl.when(at_end)
    def _():
        table_copy().start()

    def prepare(c, carry):
        for copy in input_copies(c):
            copy.wait()
        rows = pl.ds(pl.multiple_of(c * span, span), span)
        for i in range(held):
            bits = bits_in[i, rows]
            suspect = jnp.bitwise_and(bits, 1).astype(jnp.float32)
            usable = jnp.where(jnp.bitwise_and(bits, 6) == 6, 0.0, 1.0 - 0.5 * suspect)
            scaled = usable * inverse[i]
            weight = scaled.astype(jnp.bfloat16)
            weights[c, i] = weight
            weighted = (
                (scaled * pictures[i, rows].astype(jnp.float32))
                .astype(jnp.bfloat16)
                .astype(jnp.float32)
            )
            before = table[i]
            which = kernels[i]
            own_depth[i, rows] = weight.astype(jnp.float32) + own_depth[before, rows]
            sums = []
            for k in range(3):
                value = coefs[k, which] * weighted + acc[before, k, rows]
                acc[i, k, rows] = value
                sums.append(value)
            planes[i, 0, rows], planes[i, 1, rows] = split(sums[0])
            planes[i, 2, rows] = sums[1].astype(jnp.bfloat16)
            planes[i, 3, rows] = sums[2].astype(jnp.bfloat16)

        @pl.when(at_end)
        def _():
            raw_copy(c).start()

        return carry

    lax.fori_loop(0, CHUNKS, prepare, 0)

    def spill_copy(side, d):
        peer = strip + 1 if side == 0 else strip - 1
        return pltpu.make_async_remote_copy(
            src_ref=spilling.at[side, d],
            dst_ref=spilled.at[side, d],
            send_sem=spill_send.at[side, d],
            recv_sem=spill_recv.at[side, d],
            device_id={"tile": peer},
            device_id_type=MESH,
        )

    def correlate(d):
        for b in range(-1, BLOCK_COLS + 1):
            tile = d + b // BLOCK_COLS
            cols = slice((b + 1) * block, (b + 2) * block)
            for r in range(BLOCK_ROWS):
                which = last_of(table, tile, r * BLOCK_COLS + b % BLOCK_COLS)
                for k in range(4):
                    frame[k, r * block : (r + 1) * block, cols] = planes[which, k]
        first = (frame[0], frame[1])
        tall_high, tall_low = split(
            products(((down[0, 0], first[0]), (down[0, 0], first[1]), (down[1, 0], first[0])))
        )
        second = frame[2]
        tall_second = products(((down[0, 1], second), (down[1, 1], second))).astype(jnp.bfloat16)
        tall_third = products(((down[0, 2], frame[3]),)).astype(jnp.bfloat16)
        for h in range(2):
            cols = slice(h * half, h * half + half + 2 * block)
            total = products((
                (tall_high[:, cols], across[0, 0]),
                (tall_high[:, cols], across[1, 0]),
                (tall_low[:, cols], across[0, 0]),
                (tall_second[:, cols], across[0, 1]),
                (tall_second[:, cols], across[1, 1]),
                (tall_third[:, cols], across[0, 2]),
            ))
            out = slice(h * half, (h + 1) * half)
            result[d, :, out] = total[SPILL : SPILL + rows_all]
            spilling[0, d, :, out] = total[SPILL + rows_all :].astype(jnp.bfloat16)
            spilling[1, d, :, out] = total[0:SPILL].astype(jnp.bfloat16)
        for side in range(2):

            @pl.when(sends_spill[side])
            def _(side=side):
                spill_copy(side, d).start()

    def step(right, s):
        d = jnp.where(right, n - 1 - s, s)
        sends = jnp.where(right, d > me, d < me)
        gets = jnp.where(right, me > 0, me < n - 1)
        place = jnp.where(right, d, jnp.where(d == me - 1, n, d))
        return d, sends, gets, place, jnp.where(right, me + 1, me - 1)

    def arrived(ref, sems, place, c):
        pltpu.make_async_remote_copy(
            src_ref=ref.at[place, c],
            dst_ref=ref.at[place, c],
            send_sem=sems.at[place, c],
            recv_sem=sems.at[place, c],
            device_id={"band": lax.rem(band + 1, bands)},
            device_id_type=MESH,
        ).wait_recv()

    def depth_copy(right, s, c):
        d, _sends, _gets, place, target = step(right, s)
        return pltpu.make_async_remote_copy(
            src_ref=depth_moving.at[d, c],
            dst_ref=depth_moving.at[place, c],
            send_sem=depth_send.at[d, c],
            recv_sem=depth_recv.at[place, c],
            device_id={"exp": target},
            device_id_type=MESH,
        )

    def add_depth(d, c, extra):
        rows = pl.ds(pl.multiple_of(c * span, span), span)
        for r in range(BLOCK_ROWS):
            for b in range(BLOCK_COLS):
                slot = r * BLOCK_COLS + b
                cols = slice(b * block, (b + 1) * block)
                value = own_depth[last_of(table, d, slot), rows] + extra(r, slot, cols, rows)
                depth_moving[d, c, r, :, cols] = value.astype(jnp.bfloat16)

    def move_depth(right, s, c):
        d, sends, _gets, _place, _target = step(right, s)
        from_raw = jnp.where(right, gets_raw_left, gets_raw_right)

        @pl.when(sends & jnp.logical_not(at_end))
        def _():
            @pl.when(from_raw)
            def _():
                add_depth(
                    d, c,
                    lambda r, slot, cols, rows: raw_depth[last_of(raw_table, d, slot), rows],
                )

            @pl.when(jnp.logical_not(from_raw))
            def _():
                arrived(depth_moving, depth_recv, d, c)
                add_depth(
                    d, c,
                    lambda r, slot, cols, rows: depth_moving[d, c, r, :, cols].astype(jnp.float32),
                )

            depth_copy(right, s, c).start()

    def directions():
        return (left_half, jnp.logical_not(left_half))

    def depth_chunk(c):
        @pl.when(gets_raw_left | gets_raw_right)
        def _():
            @pl.when(c == 0)
            def _():
                table_copy().wait_recv()

            raw_copy(c).wait_recv()
            rows = pl.ds(pl.multiple_of(c * span, span), span)
            for i in range(held):
                raw_depth[i, rows] = raw[c, i].astype(jnp.float32) + raw_depth[raw_table[i], rows]

        def one(s, carry):
            for right in directions():
                move_depth(right, s, c)
            return carry

        lax.fori_loop(0, n - 1, one, 0)

    def complete(d):
        for side in range(2):

            @pl.when(gets_spill[side])
            def _(side=side):
                spill_copy(side, d).wait_recv()

        low = rows_all - SPILL
        result[d, 0:SPILL] += spilled[0, d].astype(jnp.float32)
        result[d, low:] += spilled[1, d].astype(jnp.float32)

    def pick(i):
        down_from = n - 1 - i
        right = jnp.where(down_from > me, down_from, down_from - 1)
        left = jnp.where(i < me, i, i + 1)
        return jnp.where(i == n - 1, me, jnp.where(left_half, right, left))

    def part_copy(right, s, q):
        d, _sends, _gets, place, target = step(right, s)
        return pltpu.make_async_remote_copy(
            src_ref=moving.at[d, q],
            dst_ref=moving.at[place, q],
            send_sem=send_sem.at[d, q],
            recv_sem=recv_sem.at[place, q],
            device_id={"exp": target},
            device_id_type=MESH,
        )

    def last_copy(q):
        target = jnp.where(me == n - 2, n - 1, 0)
        return pltpu.make_async_remote_copy(
            src_ref=last_out.at[q],
            dst_ref=last_in.at[q],
            send_sem=last_send.at[q],
            recv_sem=last_recv.at[q],
            device_id={"exp": target},
            device_id_type=MESH,
        )

    def part_rows(q):
        return pl.ds(pl.multiple_of(q * part, part), part)

    def move_first(i):
        s = i

        def one(q, carry):
            d = step(at_left, s)[0]
            moving[d, q] = result[d, part_rows(q)].astype(jnp.bfloat16)
            part_copy(at_left, s, q).start()
            return carry

        lax.fori_loop(0, PARTS, one, 0)

    def move_part(right, s, q):
        d, sends, _gets, _place, _target = step(right, s)
        to_end = jnp.where(right, me == n - 2, me == 1) & (s == 0)

        @pl.when(sends & jnp.logical_not(at_end))
        def _():
            arrived(moving, recv_sem, d, q)
            value = moving[d, q].astype(jnp.float32) + result[d, part_rows(q)]

            @pl.when(to_end)
            def _():
                last_out[q] = value
                last_copy(q).start()

            @pl.when(jnp.logical_not(to_end))
            def _():
                moving[d, q] = value.astype(jnp.bfloat16)
                part_copy(right, s, q).start()

    def turn(i, carry):
        correlate(pick(i))

        @pl.when(i > 0)
        def _():
            complete(pick(i - 1))

            @pl.when(at_end)
            def _():
                move_first(i - 1)

        @pl.when(i < CHUNKS)
        def _():
            depth_chunk(i)

        return carry

    lax.fori_loop(0, n, turn, 0)
    complete(me)
    for c in range(n, CHUNKS):
        depth_chunk(c)

    def forward(i, carry):
        for right in directions():
            move_part(right, i // PARTS, lax.rem(i, PARTS))
        return carry

    lax.fori_loop(0, (n - 1) * PARTS, forward, 0)

    def bottom(c, carry):
        chunk_rows = pl.ds(pl.multiple_of(c * span, span), span)
        for r in range(BLOCK_ROWS):
            for b in range(BLOCK_COLS):
                slot = r * BLOCK_COLS + b
                cols = slice(b * block, (b + 1) * block)
                rows = pl.ds(pl.multiple_of(r * block + c * span, span), span)
                below[rows, cols] = 1.0 + own_depth[last_of(table, me, slot), chunk_rows]

        @pl.when(gets_raw_left | gets_raw_right)
        def _():
            for r in range(BLOCK_ROWS):
                for b in range(BLOCK_COLS):
                    slot = r * BLOCK_COLS + b
                    cols = slice(b * block, (b + 1) * block)
                    rows = pl.ds(pl.multiple_of(r * block + c * span, span), span)
                    below[rows, cols] += raw_depth[last_of(raw_table, me, slot), chunk_rows]

        for has, place in (
            ((me > 1), me),
            ((me < n - 2), n),
        ):

            @pl.when(has)
            def _(place=place):
                arrived(depth_moving, depth_recv, place, c)
                for r in range(BLOCK_ROWS):
                    rows = pl.ds(pl.multiple_of(r * block + c * span, span), span)
                    below[rows] += depth_moving[place, c, r].astype(jnp.float32)

        return carry

    lax.fori_loop(0, CHUNKS, bottom, 0)

    def det_copy(j, q):
        return pltpu.make_async_remote_copy(
            src_ref=det_mine.at[part_rows(q)],
            dst_ref=det_theirs.at[j - 1, part_rows(q)],
            send_sem=det_send.at[j - 1, q],
            recv_sem=det_recv.at[j - 1, q],
            device_id={"band": lax.rem(band + j, bands)},
            device_id_type=MESH,
        )

    def finish(q, carry):
        rows = part_rows(q)

        @pl.when(at_end)
        def _():
            last_copy(q).wait_recv()
            result[me, rows] += last_in[q]

        @pl.when(jnp.logical_not(at_end))
        def _():
            arrived(moving, recv_sem, me, q)
            arrived(moving, recv_sem, n, q)
            result[me, rows] += moving[me, q].astype(jnp.float32) + moving[n, q].astype(
                jnp.float32
            )

        value = result[me, rows] / below[rows]
        coadd[rows] = value
        det_mine[rows] = value * value * below[rows]
        for j in range(1, bands):
            det_copy(j, q).start()
        return carry

    lax.fori_loop(0, PARTS, finish, 0)

    def combine(q, carry):
        rows = part_rows(q)
        value = det_mine[rows]
        for j in range(1, bands):
            det_copy(j, q).wait_recv()
            value += det_theirs[j - 1, rows]
        detection[rows] = value
        return carry

    lax.fori_loop(0, PARTS, combine, 0)

    def drain_det(q, carry):
        for j in range(1, bands):
            det_copy(j, q).wait_send()
        return carry

    lax.fori_loop(0, PARTS, drain_det, 0)

    @pl.when(at_end)
    def _():
        table_copy().wait_send()

        def drain_raw(c, carry):
            raw_copy(c).wait_send()
            return carry

        lax.fori_loop(0, CHUNKS, drain_raw, 0)

    @pl.when(jnp.logical_not(at_end))
    def _():
        def drain_depth(i, carry):
            s, c = i // CHUNKS, lax.rem(i, CHUNKS)
            for right in directions():

                @pl.when(step(right, s)[1])
                def _(right=right):
                    depth_copy(right, s, c).wait_send()

            return carry

        lax.fori_loop(0, (n - 1) * CHUNKS, drain_depth, 0)

    def drain(i, carry):
        s, q = i // PARTS, lax.rem(i, PARTS)
        for right in directions():
            to_end = jnp.where(right, me == n - 2, me == 1) & (s == 0)
            sends = step(right, s)[1]

            @pl.when(sends & to_end)
            def _():
                last_copy(q).wait_send()

            @pl.when(sends & jnp.logical_not(to_end))
            def _(right=right):
                part_copy(right, s, q).wait_send()

        return carry

    lax.fori_loop(0, (n - 1) * PARTS, drain, 0)

    def drain_spill(d, carry):
        for side in range(2):

            @pl.when(sends_spill[side])
            def _(side=side):
                spill_copy(side, d).wait_send()

        return carry

    lax.fori_loop(0, n, drain_spill, 0)


def local(sizes, images, mask_bits, inv_var, routes, block_slot, kernel_index, coefficients):
    n, strips, bands = sizes["exp"], sizes["tile"], sizes["band"]
    held, block = images.shape[2:4]
    tile_rows = BLOCK_ROWS * block
    tile_cols = BLOCK_COLS * block
    half = tile_cols // 2
    span = block // CHUNKS
    part = tile_rows // PARTS
    entries = pl.cdiv(held + (n + 2) * SLOTS, 128) * 128
    across = tap_pair(tap_matrix(2 * half, half, block))
    down = tap_pair(tap_matrix(tile_rows + 2 * SPILL, tile_rows, SPILL))
    smem = pl.BlockSpec(memory_space=pltpu.SMEM)
    vmem = pl.BlockSpec(memory_space=pltpu.VMEM)
    anywhere = pl.BlockSpec(memory_space=pl.ANY)
    whole = jax.ShapeDtypeStruct((tile_rows, tile_cols), jnp.float32)
    bf16, f32 = jnp.bfloat16, jnp.float32
    dma = pltpu.SemaphoreType.DMA
    coadd, detection = pl.pallas_call(
        functools.partial(coadd_kernel, n, strips, bands),
        out_shape=(whole, whole),
        in_specs=[smem] * 5 + [anywhere] * 2 + [vmem] * 2,
        out_specs=(vmem, vmem),
        scratch_shapes=[
            pltpu.VMEM((held, block, block), bf16),
            pltpu.VMEM((held, block, block), jnp.int32),
            pltpu.VMEM((CHUNKS, held, span, block), bf16),
            pltpu.VMEM((CHUNKS, held, span, block), bf16),
            pltpu.VMEM((held + 1, 3, block, block), f32),
            pltpu.VMEM((held + 1, 4, block, block), bf16),
            pltpu.VMEM((held + 1, block, block), f32),
            pltpu.VMEM((held + 1, block, block), f32),
            pltpu.SMEM((entries,), jnp.int32),
            pltpu.SMEM((entries,), jnp.int32),
            pltpu.VMEM((4, tile_rows, tile_cols + 2 * block), bf16),
            pltpu.VMEM((n, tile_rows, tile_cols), f32),
            pltpu.VMEM((n + 1, CHUNKS, BLOCK_ROWS, span, tile_cols), bf16),
            pltpu.VMEM((n + 1, PARTS, part, tile_cols), bf16),
            pltpu.VMEM((PARTS, part, tile_cols), f32),
            pltpu.VMEM((PARTS, part, tile_cols), f32),
            pltpu.VMEM((2, n, SPILL, tile_cols), bf16),
            pltpu.VMEM((2, n, SPILL, tile_cols), bf16),
            pltpu.VMEM((tile_rows, tile_cols), f32),
            pltpu.VMEM((tile_rows, tile_cols), f32),
            pltpu.VMEM((bands - 1, tile_rows, tile_cols), f32),
            dma((CHUNKS, 2)),
            dma((CHUNKS,)),
            dma((CHUNKS,)),
            dma((2,)),
            dma((n, CHUNKS)),
            dma((n + 1, CHUNKS)),
            dma((n, PARTS)),
            dma((n + 1, PARTS)),
            dma((PARTS,)),
            dma((PARTS,)),
            dma((2, n)),
            dma((2, n)),
            dma((bands - 1, PARTS)),
            dma((bands - 1, PARTS)),
        ],
        compiler_params=pltpu.CompilerParams(collective_id=0, has_side_effects=True),
        name="coadd",
    )(
        routes[0, 0, :, 0], block_slot[0, 0], kernel_index[0, 0], inv_var[0, 0],
        coefficients.T, images[0, 0], mask_bits[0, 0], across, down,
    )
    return coadd[None], detection


def solution(mesh):
    return jax.shard_map(
        functools.partial(local, dict(mesh.shape)),
        mesh=mesh,
        in_specs=(
            P(("patch", "band"), "tile", "exp", None, None),
            P(("patch", "band"), "tile", "exp", None, None),
            P(("patch", "band"), "tile", "exp"),
            P(("patch", "band"), "tile", "exp", None),
            P(("patch", "band"), "tile", "exp"),
            P(("patch", "band"), "tile", "exp"),
            P(),
        ),
        out_specs=(P(("patch", "band"), "tile", "exp"), P(("patch", "tile"), "exp")),
        check_vma=False,
    )
```

time: 59.5 us -> 60.5 us (1.017)
  local copies, waits for them, and re-layouts: 0 us -> 3.74 us
  Pallas kernels: 58.6 us -> 55.9 us
    unnamed x0 -> x2, local copies, waits for them, and re-layouts: none -> 3.74 us
    pallas_call x3 -> x1, Pallas kernels: 58.6 us -> 55.9 us  [local(): pl.pallas_call(functools.partial(coadd_kernel, n, strips, bands), out_sha...]
where the time goes in v1:
time: 60.5 us; the launch traced here: 60.3 us
  Pallas kernels  55.9 us (92%)
  local copies, waits for them, and re-layouts  3.74 us (6%)
  between operations  0.64 us (1%)
    pallas_call x1, Pallas kernels, local(): pl.pallas_call(functools.partial(coadd_kernel, n, strips, bands), out_sha...  55.9 us
    unnamed x2, local copies, waits for them, and re-layouts  3.74 us

profile of v1, /device:TPU:9, one launch (start us, length us, event | category | flops | bytes accessed | tf_op | source)
XLA Modules:
  0.0 60.3 jit_solution(5470904429762916401)
XLA Ops:
  0.6 55.9 %coadd.1 = (f32[256,512]{1,0:T(8,128)}, f32[256,512]{1,0:T(8,128)}) custom-call(s32[16]{0:T(128)} %bitcast.12, s32[16]{0:T(128)} %bitcast.13, s32[16]{0:T(128)} %bitcast.14, f32[16]{0:T(128)} %bitcast.15, f32[3,64]{1,0:T(4,128)} %bitcast.11, bf16[16,128,128]{2,1,0:T(8,128)(2,1)} %bitcast.9, s32[16,128,128]{2,1,0:T(8,128)} %bitcast.8, ...), custom_call_target="tpu_custom_call" | custom-call | tf_op jit(solution)/shard_map/coadd/pallas_call | solution.py:600
  56.5 1.9 %copy.13 = f32[1,256,512]{2,1,0:T(8,128)} copy(f32[1,256,512]{2,1,0:T(8,128)} %bitcast.10) | data formatting | bytes 1048576
  58.4 1.9 %copy.14 = f32[256,512]{1,0:T(8,128)} copy(f32[256,512]{1,0:T(8,128)} %get-tuple-element.9) | data formatting | bytes 1048576

commit v2 on v1

--- a/solution.py
+++ b/solution.py
@@ -59,12 +59,12 @@
 
 def coadd_kernel(
     n, strips, bands,
-    routes, slots, kernels, inverse, coefs, images, masks, across, down,
+    routes, slots, kernels, inverse, coefs, images, masks, across_in, down_in,
     coadd, detection,
-    pictures, bits_in, weights, raw, acc, planes, own_depth, raw_depth, table, raw_table,
+    across, down, pictures, bits_in, weights, raw, acc, planes, own_depth, raw_depth, table, raw_table,
     frame, result, depth_moving, moving, last_out, last_in, spilling, spilled,
     below, det_mine, det_theirs,
-    in_sem, raw_send, raw_recv, table_sem, depth_send, depth_recv, send_sem, recv_sem,
+    taps_sem, in_sem, raw_send, raw_recv, table_sem, depth_send, depth_recv, send_sem, recv_sem,
     last_send, last_recv, spill_send, spill_recv, det_send, det_recv,
 ):
     me = lax.axis_index("exp")
@@ -91,6 +91,13 @@
         for copy in input_copies(c):
             copy.start()
 
+    taps_copies = (
+        pltpu.make_async_copy(down_in, down, taps_sem.at[0]),
+        pltpu.make_async_copy(across_in, across, taps_sem.at[1]),
+    )
+    for copy in taps_copies:
+        copy.start()
+
     barrier = pltpu.get_barrier_semaphore()
     greet = [
         (strip > 0, {"tile": strip - 1}),
@@ -146,8 +153,6 @@
         def _(side=side):
             spilled[side] = jnp.zeros(spilled.shape[1:], spilled.dtype)
 
-    pl.semaphore_wait(barrier, peers)
-
     inward = jnp.where(at_left, 1, n - 2)
 
     def raw_copy(c):
@@ -170,21 +175,33 @@
             device_id_type=MESH,
         )
 
+    def scaled_of(i, rows):
+        bits = bits_in[i, rows]
+        suspect = jnp.bitwise_and(bits, 1).astype(jnp.float32)
+        usable = jnp.where(jnp.bitwise_and(bits, 6) == 6, 0.0, 1.0 - 0.5 * suspect)
+        return usable * inverse[i]
+
+    def weigh(c, carry):
+        input_copies(c)[0].wait()
+        rows = pl.ds(pl.multiple_of(c * span, span), span)
+        for i in range(held):
+            weights[c, i] = scaled_of(i, rows).astype(jnp.bfloat16)
+        return carry
+
+    lax.fori_loop(0, CHUNKS, weigh, 0)
+    pl.semaphore_wait(barrier, peers)
+
     @pl.when(at_end)
     def _():
+        for c in range(CHUNKS):
+            raw_copy(c).start()
         table_copy().start()
 
     def prepare(c, carry):
-        for copy in input_copies(c):
-            copy.wait()
+        input_copies(c)[1].wait()
         rows = pl.ds(pl.multiple_of(c * span, span), span)
         for i in range(held):
-            bits = bits_in[i, rows]
-            suspect = jnp.bitwise_and(bits, 1).astype(jnp.float32)
-            usable = jnp.where(jnp.bitwise_and(bits, 6) == 6, 0.0, 1.0 - 0.5 * suspect)
-            scaled = usable * inverse[i]
-            weight = scaled.astype(jnp.bfloat16)
-            weights[c, i] = weight
+            scaled = scaled_of(i, rows)
             weighted = (
                 (scaled * pictures[i, rows].astype(jnp.float32))
                 .astype(jnp.bfloat16)
@@ -192,7 +209,7 @@
             )
             before = table[i]
             which = kernels[i]
-            own_depth[i, rows] = weight.astype(jnp.float32) + own_depth[before, rows]
+            own_depth[i, rows] = weights[c, i].astype(jnp.float32) + own_depth[before, rows]
             sums = []
             for k in range(3):
                 value = coefs[k, which] * weighted + acc[before, k, rows]
@@ -202,13 +219,12 @@
             planes[i, 2, rows] = sums[1].astype(jnp.bfloat16)
             planes[i, 3, rows] = sums[2].astype(jnp.bfloat16)
 
-        @pl.when(at_end)
-        def _():
-            raw_copy(c).start()
-
         return carry
 
     lax.fori_loop(0, CHUNKS, prepare, 0)
+
+    for copy in taps_copies:
+        copy.wait()
 
     def spill_copy(side, d):
         peer = strip + 1 if side == 0 else strip - 1
@@ -319,21 +335,29 @@
     def directions():
         return (left_half, jnp.logical_not(left_half))
 
-    def depth_chunk(c):
-        @pl.when(gets_raw_left | gets_raw_right)
+    def lag(right):
+        return jnp.where(right, me - 1, n - 2 - me)
+
+    def depth_slot(t):
+        @pl.when((gets_raw_left | gets_raw_right) & (t < CHUNKS))
         def _():
-            @pl.when(c == 0)
+            @pl.when(t == 0)
             def _():
                 table_copy().wait_recv()
 
-            raw_copy(c).wait_recv()
-            rows = pl.ds(pl.multiple_of(c * span, span), span)
+            raw_copy(t).wait_recv()
+            rows = pl.ds(pl.multiple_of(t * span, span), span)
             for i in range(held):
-                raw_depth[i, rows] = raw[c, i].astype(jnp.float32) + raw_depth[raw_table[i], rows]
+                raw_depth[i, rows] = raw[t, i].astype(jnp.float32) + raw_depth[raw_table[i], rows]
 
         def one(s, carry):
             for right in directions():
-                move_depth(right, s, c)
+                c = t - lag(right)
+
+                @pl.when((c >= 0) & (c < CHUNKS))
+                def _(right=right, c=c):
+                    move_depth(right, s, c)
+
             return carry
 
         lax.fori_loop(0, n - 1, one, 0)
@@ -421,23 +445,25 @@
             def _():
                 move_first(i - 1)
 
-        @pl.when(i < CHUNKS)
-        def _():
-            depth_chunk(i)
-
+        depth_slot(i)
         return carry
 
     lax.fori_loop(0, n, turn, 0)
     complete(me)
-    for c in range(n, CHUNKS):
-        depth_chunk(c)
-
-    def forward(i, carry):
+    for t in range(n, CHUNKS + n - 3):
+        depth_slot(t)
+
+    def forward(t, carry):
         for right in directions():
-            move_part(right, i // PARTS, lax.rem(i, PARTS))
-        return carry
-
-    lax.fori_loop(0, (n - 1) * PARTS, forward, 0)
+            i = t - lag(right)
+
+            @pl.when((i >= 0) & (i < (n - 1) * PARTS))
+            def _(right=right, i=i):
+                move_part(right, i // PARTS, lax.rem(i, PARTS))
+
+        return carry
+
+    lax.fori_loop(0, (n - 1) * PARTS + n - 3, forward, 0)
 
     def bottom(c, carry):
         chunk_rows = pl.ds(pl.multiple_of(c * span, span), span)
@@ -593,58 +619,71 @@
     down = tap_pair(tap_matrix(tile_rows + 2 * SPILL, tile_rows, SPILL))
     smem = pl.BlockSpec(memory_space=pltpu.SMEM)
     vmem = pl.BlockSpec(memory_space=pltpu.VMEM)
-    anywhere = pl.BlockSpec(memory_space=pl.ANY)
+    anywhere = pl.BlockSpec(memory_space=pltpu.HBM)
     whole = jax.ShapeDtypeStruct((tile_rows, tile_cols), jnp.float32)
     bf16, f32 = jnp.bfloat16, jnp.float32
     dma = pltpu.SemaphoreType.DMA
+    scratch = [
+        pltpu.VMEM(across.shape, bf16),
+        pltpu.VMEM(down.shape, bf16),
+        pltpu.VMEM((held, block, block), bf16),
+        pltpu.VMEM((held, block, block), jnp.int32),
+        pltpu.VMEM((CHUNKS, held, span, block), bf16),
+        pltpu.VMEM((CHUNKS, held, span, block), bf16),
+        pltpu.VMEM((held + 1, 3, block, block), f32),
+        pltpu.VMEM((held + 1, 4, block, block), bf16),
+        pltpu.VMEM((held + 1, block, block), f32),
+        pltpu.VMEM((held + 1, block, block), f32),
+        pltpu.SMEM((entries,), jnp.int32),
+        pltpu.SMEM((entries,), jnp.int32),
+        pltpu.VMEM((4, tile_rows, tile_cols + 2 * block), bf16),
+        pltpu.VMEM((n, tile_rows, tile_cols), f32),
+        pltpu.VMEM((n + 1, CHUNKS, BLOCK_ROWS, span, tile_cols), bf16),
+        pltpu.VMEM((n + 1, PARTS, part, tile_cols), bf16),
+        pltpu.VMEM((PARTS, part, tile_cols), f32),
+        pltpu.VMEM((PARTS, part, tile_cols), f32),
+        pltpu.VMEM((2, n, SPILL, tile_cols), bf16),
+        pltpu.VMEM((2, n, SPILL, tile_cols), bf16),
+        pltpu.VMEM((tile_rows, tile_cols), f32),
+        pltpu.VMEM((tile_rows, tile_cols), f32),
+        pltpu.VMEM((bands - 1, tile_rows, tile_cols), f32),
+        dma((2,)),
+        dma((CHUNKS, 2)),
+        dma((CHUNKS,)),
+        dma((CHUNKS,)),
+        dma((2,)),
+        dma((n, CHUNKS)),
+        dma((n + 1, CHUNKS)),
+        dma((n, PARTS)),
+        dma((n + 1, PARTS)),
+        dma((PARTS,)),
+        dma((PARTS,)),
+        dma((2, n)),
+        dma((2, n)),
+        dma((bands - 1, PARTS)),
+        dma((bands - 1, PARTS)),
+    ]
+    held_bytes = sum(
+        int(np.prod(x.shape)) * jnp.dtype(x.dtype).itemsize
+        for x in scratch
+        if x.memory_space == pltpu.VMEM
+    )
+    limit = min(held_bytes + (16 << 20), 60 * 1024 * 1024)
     coadd, detection = pl.pallas_call(
         functools.partial(coadd_kernel, n, strips, bands),
         out_shape=(whole, whole),
-        in_specs=[smem] * 5 + [anywhere] * 2 + [vmem] * 2,
+        in_specs=[smem] * 5 + [anywhere] * 4,
         out_specs=(vmem, vmem),
-        scratch_shapes=[
-            pltpu.VMEM((held, block, block), bf16),
-            pltpu.VMEM((held, block, block), jnp.int32),
-            pltpu.VMEM((CHUNKS, held, span, block), bf16),
-            pltpu.VMEM((CHUNKS, held, span, block), bf16),
-            pltpu.VMEM((held + 1, 3, block, block), f32),
-            pltpu.VMEM((held + 1, 4, block, block), bf16),
-            pltpu.VMEM((held + 1, block, block), f32),
-            pltpu.VMEM((held + 1, block, block), f32),
-            pltpu.SMEM((entries,), jnp.int32),
-            pltpu.SMEM((entries,), jnp.int32),
-            pltpu.VMEM((4, tile_rows, tile_cols + 2 * block), bf16),
-            pltpu.VMEM((n, tile_rows, tile_cols), f32),
-            pltpu.VMEM((n + 1, CHUNKS, BLOCK_ROWS, span, tile_cols), bf16),
-            pltpu.VMEM((n + 1, PARTS, part, tile_cols), bf16),
-            pltpu.VMEM((PARTS, part, tile_cols), f32),
-            pltpu.VMEM((PARTS, part, tile_cols), f32),
-            pltpu.VMEM((2, n, SPILL, tile_cols), bf16),
-            pltpu.VMEM((2, n, SPILL, tile_cols), bf16),
-            pltpu.VMEM((tile_rows, tile_cols), f32),
-            pltpu.VMEM((tile_rows, tile_cols), f32),
-            pltpu.VMEM((bands - 1, tile_rows, tile_cols), f32),
-            dma((CHUNKS, 2)),
-            dma((CHUNKS,)),
-            dma((CHUNKS,)),
-            dma((2,)),
-            dma((n, CHUNKS)),
-            dma((n + 1, CHUNKS)),
-            dma((n, PARTS)),
-            dma((n + 1, PARTS)),
-            dma((PARTS,)),
-            dma((PARTS,)),
-            dma((2, n)),
-            dma((2, n)),
-            dma((bands - 1, PARTS)),
-            dma((bands - 1, PARTS)),
-        ],
-        compiler_params=pltpu.CompilerParams(collective_id=0, has_side_effects=True),
+        scratch_shapes=scratch,
+        compiler_params=pltpu.CompilerParams(collective_id=0, has_side_effects=True, vmem_limit_bytes=limit),
         name="coadd",
-    )(
-        routes[0, 0, :, 0], block_slot[0, 0], kernel_index[0, 0], inv_var[0, 0],
-        coefficients.T, images[0, 0], mask_bits[0, 0], across, down,
-    )
+    )(*[
+        pltpu.with_memory_space_constraint(x, pltpu.HBM)
+        for x in (
+            routes[0, 0, :, 0], block_slot[0, 0], kernel_index[0, 0], inv_var[0, 0],
+            coefficients.T, images[0, 0], mask_bits[0, 0], across, down,
+        )
+    ])
     return coadd[None], detection
 
 

time: 60.5 us -> 50.9 us (0.84)
  the two profiles are of different devices: /device:TPU:9 before, /device:TPU:0 now
where the time goes in v2:
time: 50.9 us; the launch traced here: 50.7 us
  Pallas kernels  48.5 us (95%)
  local copies, waits for them, and re-layouts  1.59 us (3%)
  between operations  0.64 us (1%)
    pallas_call x1, Pallas kernels, local(): pl.pallas_call(functools.partial(coadd_kernel, n, strips, bands), out_sha...  48.5 us
    unnamed x2, local copies, waits for them, and re-layouts  1.59 us

profile of v2, /device:TPU:0, one launch (start us, length us, event | category | flops | bytes accessed | tf_op | source)
XLA Modules:
  0.0 50.7 jit_solution(12767796679645721388)
XLA Ops:
  0.6 48.5 %coadd.1 = (f32[256,512]{1,0:T(8,128)S(1)}, f32[256,512]{1,0:T(8,128)S(1)}) custom-call(s32[16]{0:T(128)} %bitcast.12, s32[16]{0:T(128)} %bitcast.13, s32[16]{0:T(128)} %bitcast.14, f32[16]{0:T(128)} %bitcast.15, f32[3,64]{1,0:T(4,128)} %bitcast.11, bf16[16,128,128]{2,1,0:T(8,128)(2,1)} %bitcast.10, s32[16,128,128]{2,1,0:T(8,128)} %bitcast.9, ...), custom_call_target="tpu_custom_call" | custom-call | tf_op jit(solution)/shard_map/coadd/pallas_call | solution.py:672
  49.1 0.8 %copy.13 = f32[1,256,512]{2,1,0:T(8,128)} copy(f32[1,256,512]{2,1,0:T(8,128)S(1)} %bitcast.8) | data formatting | bytes 1048576
  49.9 0.8 %copy.14 = f32[256,512]{1,0:T(8,128)} copy(f32[256,512]{1,0:T(8,128)S(1)} %get-tuple-element.9) | data formatting | bytes 1048576

commit v3 on v2

--- a/solution.py
+++ b/solution.py
@@ -14,7 +14,8 @@
 SLOTS = BLOCK_ROWS * BLOCK_COLS
 SPILL = 24
 CHUNKS = 4
-PARTS = 4
+PARTS = 8
+LAG = 2
 
 kernel_sigmas = (1.0, 2.5, 6.0)
 MESH = pl.DeviceIdType.MESH
@@ -118,40 +119,8 @@
             barrier, inc=1, device_id={"band": lax.rem(band + j, bands)}, device_id_type=MESH
         )
 
-    keys = [routes[i] * SLOTS + slots[i] for i in range(held)]
-    for i in range(held):
-        before = held
-        for j in range(i):
-            before = jnp.where(keys[j] == keys[i], j, before)
-        table[i] = jnp.int32(before)
-
-    def note_last(key, carry):
-        last = held
-        for i in range(held):
-            last = jnp.where(routes[i] * SLOTS + slots[i] == key - SLOTS, i, last)
-        table[held + key] = last
-        return carry
-
-    lax.fori_loop(0, (n + 2) * SLOTS, note_last, 0)
-
     def last_of(entries, d, slot):
         return entries[held + (d + 1) * SLOTS + slot]
-
-    none = jnp.zeros((block, block), jnp.float32)
-    for k in range(3):
-        acc[held, k] = none
-    for k in range(4):
-        planes[held, k] = none.astype(jnp.bfloat16)
-    own_depth[held] = none
-    raw_depth[held] = none
-
-    sends_spill = (strip < strips - 1, strip > 0)
-    gets_spill = (strip > 0, strip < strips - 1)
-    for side in range(2):
-
-        @pl.when(jnp.logical_not(gets_spill[side]))
-        def _(side=side):
-            spilled[side] = jnp.zeros(spilled.shape[1:], spilled.dtype)
 
     inward = jnp.where(at_left, 1, n - 2)
 
@@ -188,14 +157,60 @@
             weights[c, i] = scaled_of(i, rows).astype(jnp.bfloat16)
         return carry
 
-    lax.fori_loop(0, CHUNKS, weigh, 0)
+    weigh(0, 0)
     pl.semaphore_wait(barrier, peers)
 
     @pl.when(at_end)
     def _():
-        for c in range(CHUNKS):
+        raw_copy(0).start()
+
+    keys = [routes[i] * SLOTS + slots[i] for i in range(held)]
+    for i in range(held):
+        before = held
+        for j in range(i):
+            before = jnp.where(keys[j] == keys[i], j, before)
+        table[i] = jnp.int32(before)
+
+    def note_last(key, carry):
+        last = held
+        for i in range(held):
+            last = jnp.where(routes[i] * SLOTS + slots[i] == key - SLOTS, i, last)
+        table[held + key] = last
+        return carry
+
+    lax.fori_loop(0, (n + 2) * SLOTS, note_last, 0)
+
+    @pl.when(at_end)
+    def _():
+        table_copy().start()
+
+    def weigh_and_send(c, carry):
+        weigh(c, 0)
+
+        @pl.when(at_end)
+        def _():
             raw_copy(c).start()
-        table_copy().start()
+
+        return carry
+
+    lax.fori_loop(1, CHUNKS, weigh_and_send, 0)
+
+    none = jnp.zeros((block, block), jnp.float32)
+    for k in range(3):
+        acc[held, k] = none
+    for k in range(4):
+        planes[held, k] = none.astype(jnp.bfloat16)
+    own_depth[held] = none
+    raw_depth[held] = none
+
+    sends_spill = (strip < strips - 1, strip > 0)
+    gets_spill = (strip > 0, strip < strips - 1)
+    for side in range(2):
+
+        @pl.when(jnp.logical_not(gets_spill[side]))
+        def _(side=side):
+            spilled[side] = jnp.zeros(spilled.shape[1:], spilled.dtype)
+
 
     def prepare(c, carry):
         input_copies(c)[1].wait()
@@ -336,7 +351,7 @@
         return (left_half, jnp.logical_not(left_half))
 
     def lag(right):
-        return jnp.where(right, me - 1, n - 2 - me)
+        return LAG * jnp.where(right, me - 1, n - 2 - me)
 
     def depth_slot(t):
         @pl.when((gets_raw_left | gets_raw_right) & (t < CHUNKS))
@@ -434,6 +449,8 @@
                 moving[d, q] = value.astype(jnp.bfloat16)
                 part_copy(right, s, q).start()
 
+    per_turn = pl.cdiv(CHUNKS, n)
+
     def turn(i, carry):
         correlate(pick(i))
 
@@ -445,13 +462,18 @@
             def _():
                 move_first(i - 1)
 
-        depth_slot(i)
+        for k in range(per_turn):
+            depth_slot(i * per_turn + k)
         return carry
 
     lax.fori_loop(0, n, turn, 0)
     complete(me)
-    for t in range(n, CHUNKS + n - 3):
+
+    def late_slot(t, carry):
         depth_slot(t)
+        return carry
+
+    lax.fori_loop(n * per_turn, CHUNKS + LAG * (n - 3), late_slot, 0)
 
     def forward(t, carry):
         for right in directions():
@@ -463,7 +485,7 @@
 
         return carry
 
-    lax.fori_loop(0, (n - 1) * PARTS + n - 3, forward, 0)
+    lax.fori_loop(0, (n - 1) * PARTS + LAG * (n - 3), forward, 0)
 
     def bottom(c, carry):
         chunk_rows = pl.ds(pl.multiple_of(c * span, span), span)
@@ -534,6 +556,59 @@
 
     lax.fori_loop(0, PARTS, finish, 0)
 
+    @pl.when(at_end)
+    def _():
+        table_copy().wait_send()
+
+        def drain_raw(c, carry):
+            raw_copy(c).wait_send()
+            return carry
+
+        lax.fori_loop(0, CHUNKS, drain_raw, 0)
+
+    @pl.when(jnp.logical_not(at_end))
+    def _():
+        def drain_depth(i, carry):
+            s, c = i // CHUNKS, lax.rem(i, CHUNKS)
+            for right in directions():
+
+                @pl.when(step(right, s)[1])
+                def _(right=right):
+                    depth_copy(right, s, c).wait_send()
+
+            return carry
+
+        lax.fori_loop(0, (n - 1) * CHUNKS, drain_depth, 0)
+
+    def drain(i, carry):
+        s, q = i // PARTS, lax.rem(i, PARTS)
+        for right in directions():
+            to_end = jnp.where(right, me == n - 2, me == 1) & (s == 0)
+            sends = step(right, s)[1]
+
+            @pl.when(sends & to_end)
+            def _():
+                last_copy(q).wait_send()
+
+            @pl.when(sends & jnp.logical_not(to_end))
+            def _(right=right):
+                part_copy(right, s, q).wait_send()
+
+        return carry
+
+    lax.fori_loop(0, (n - 1) * PARTS, drain, 0)
+
+    def drain_spill(d, carry):
+        for side in range(2):
+
+            @pl.when(sends_spill[side])
+            def _(side=side):
+                spill_copy(side, d).wait_send()
+
+        return carry
+
+    lax.fori_loop(0, n, drain_spill, 0)
+
     def combine(q, carry):
         rows = part_rows(q)
         value = det_mine[rows]
@@ -551,59 +626,6 @@
         return carry
 
     lax.fori_loop(0, PARTS, drain_det, 0)
-
-    @pl.when(at_end)
-    def _():
-        table_copy().wait_send()
-
-        def drain_raw(c, carry):
-            raw_copy(c).wait_send()
-            return carry
-
-        lax.fori_loop(0, CHUNKS, drain_raw, 0)
-
-    @pl.when(jnp.logical_not(at_end))
-    def _():
-        def drain_depth(i, carry):
-            s, c = i // CHUNKS, lax.rem(i, CHUNKS)
-            for right in directions():
-
-                @pl.when(step(right, s)[1])
-                def _(right=right):
-                    depth_copy(right, s, c).wait_send()
-
-            return carry
-
-        lax.fori_loop(0, (n - 1) * CHUNKS, drain_depth, 0)
-
-    def drain(i, carry):
-        s, q = i // PARTS, lax.rem(i, PARTS)
-        for right in directions():
-            to_end = jnp.where(right, me == n - 2, me == 1) & (s == 0)
-            sends = step(right, s)[1]
-
-            @pl.when(sends & to_end)
-            def _():
-                last_copy(q).wait_send()
-
-            @pl.when(sends & jnp.logical_not(to_end))
-            def _(right=right):
-                part_copy(right, s, q).wait_send()
-
-        return carry
-
-    lax.fori_loop(0, (n - 1) * PARTS, drain, 0)
-
-    def drain_spill(d, carry):
-        for side in range(2):
-
-            @pl.when(sends_spill[side])
-            def _(side=side):
-                spill_copy(side, d).wait_send()
-
-        return carry
-
-    lax.fori_loop(0, n, drain_spill, 0)
 
 
 def local(sizes, images, mask_bits, inv_var, routes, block_slot, kernel_index, coefficients):

time: 50.9 us -> 41.9 us (0.82)
  Pallas kernels: 48.5 us -> 39.5 us
    pallas_call x1, Pallas kernels: 48.5 us -> 39.5 us  [local(): pl.pallas_call(functools.partial(coadd_kernel, n, strips, bands), out_sha...]
where the time goes in v3:
time: 41.9 us; the launch traced here: 41.7 us
  Pallas kernels  39.5 us (94%)
  local copies, waits for them, and re-layouts  1.59 us (4%)
  between operations  0.64 us (2%)
    pallas_call x1, Pallas kernels, local(): pl.pallas_call(functools.partial(coadd_kernel, n, strips, bands), out_sha...  39.5 us
    unnamed x2, local copies, waits for them, and re-layouts  1.59 us

profile of v3, /device:TPU:0, one launch (start us, length us, event | category | flops | bytes accessed | tf_op | source)
XLA Modules:
  0.0 41.7 jit_solution(6894487009330552392)
XLA Ops:
  0.6 39.5 %coadd.1 = (f32[256,512]{1,0:T(8,128)S(1)}, f32[256,512]{1,0:T(8,128)S(1)}) custom-call(s32[16]{0:T(128)} %bitcast.12, s32[16]{0:T(128)} %bitcast.13, s32[16]{0:T(128)} %bitcast.14, f32[16]{0:T(128)} %bitcast.15, f32[3,64]{1,0:T(4,128)} %bitcast.11, bf16[16,128,128]{2,1,0:T(8,128)(2,1)} %bitcast.10, s32[16,128,128]{2,1,0:T(8,128)} %bitcast.9, ...), custom_call_target="tpu_custom_call" | custom-call | tf_op jit(solution)/shard_map/coadd/pallas_call | solution.py:694
  40.1 0.8 %copy.13 = f32[1,256,512]{2,1,0:T(8,128)} copy(f32[1,256,512]{2,1,0:T(8,128)S(1)} %bitcast.8) | data formatting | bytes 1048576
  40.9 0.8 %copy.14 = f32[256,512]{1,0:T(8,128)} copy(f32[256,512]{1,0:T(8,128)S(1)} %get-tuple-element.9) | data formatting | bytes 1048576

commit v4 on v3

--- a/solution.py
+++ b/solution.py
@@ -15,7 +15,9 @@
 SPILL = 24
 CHUNKS = 4
 PARTS = 8
-LAG = 2
+STRIDE = 4
+EARLY = 3
+LAG = 6
 
 kernel_sigmas = (1.0, 2.5, 6.0)
 MESH = pl.DeviceIdType.MESH
@@ -61,12 +63,12 @@
 def coadd_kernel(
     n, strips, bands,
     routes, slots, kernels, inverse, coefs, images, masks, across_in, down_in,
-    coadd, detection,
-    across, down, pictures, bits_in, weights, raw, acc, planes, own_depth, raw_depth, table, raw_table,
+    coadd_out, detection_out,
+    coadd, detection, across, down, pictures, bits_in, weights, raw, acc, planes, own_depth, raw_depth, table, raw_table,
     frame, result, depth_moving, moving, last_out, last_in, spilling, spilled,
     below, det_mine, det_theirs,
     taps_sem, in_sem, raw_send, raw_recv, table_sem, depth_send, depth_recv, send_sem, recv_sem,
-    last_send, last_recv, spill_send, spill_recv, det_send, det_recv,
+    last_send, last_recv, spill_send, spill_recv, det_send, det_recv, out_sem,
 ):
     me = lax.axis_index("exp")
     strip = lax.axis_index("tile")
@@ -128,7 +130,7 @@
         return pltpu.make_async_remote_copy(
             src_ref=weights.at[c],
             dst_ref=raw.at[c],
-            send_sem=raw_send.at[c],
+            send_sem=raw_send.at[0],
             recv_sem=raw_recv.at[c],
             device_id={"exp": inward},
             device_id_type=MESH,
@@ -193,7 +195,9 @@
 
         return carry
 
-    lax.fori_loop(1, CHUNKS, weigh_and_send, 0)
+    lax.fori_loop(1, EARLY, weigh_and_send, 0)
+    for c in range(EARLY, CHUNKS):
+        weigh(c, 0)
 
     none = jnp.zeros((block, block), jnp.float32)
     for k in range(3):
@@ -246,7 +250,7 @@
         return pltpu.make_async_remote_copy(
             src_ref=spilling.at[side, d],
             dst_ref=spilled.at[side, d],
-            send_sem=spill_send.at[side, d],
+            send_sem=spill_send.at[side],
             recv_sem=spill_recv.at[side, d],
             device_id={"tile": peer},
             device_id_type=MESH,
@@ -309,7 +313,7 @@
         return pltpu.make_async_remote_copy(
             src_ref=depth_moving.at[d, c],
             dst_ref=depth_moving.at[place, c],
-            send_sem=depth_send.at[d, c],
+            send_sem=depth_send.at[d],
             recv_sem=depth_recv.at[place, c],
             device_id={"exp": target},
             device_id_type=MESH,
@@ -353,29 +357,15 @@
     def lag(right):
         return LAG * jnp.where(right, me - 1, n - 2 - me)
 
-    def depth_slot(t):
-        @pl.when((gets_raw_left | gets_raw_right) & (t < CHUNKS))
-        def _():
-            @pl.when(t == 0)
-            def _():
-                table_copy().wait_recv()
-
-            raw_copy(t).wait_recv()
-            rows = pl.ds(pl.multiple_of(t * span, span), span)
-            for i in range(held):
-                raw_depth[i, rows] = raw[t, i].astype(jnp.float32) + raw_depth[raw_table[i], rows]
-
-        def one(s, carry):
-            for right in directions():
-                c = t - lag(right)
-
-                @pl.when((c >= 0) & (c < CHUNKS))
-                def _(right=right, c=c):
-                    move_depth(right, s, c)
-
-            return carry
-
-        lax.fori_loop(0, n - 1, one, 0)
+    def take_raw(c):
+        @pl.when(c == 0)
+        def _():
+            table_copy().wait_recv()
+
+        raw_copy(c).wait_recv()
+        rows = pl.ds(pl.multiple_of(c * span, span), span)
+        for i in range(held):
+            raw_depth[i, rows] = raw[c, i].astype(jnp.float32) + raw_depth[raw_table[i], rows]
 
     def complete(d):
         for side in range(2):
@@ -399,7 +389,7 @@
         return pltpu.make_async_remote_copy(
             src_ref=moving.at[d, q],
             dst_ref=moving.at[place, q],
-            send_sem=send_sem.at[d, q],
+            send_sem=send_sem.at[d],
             recv_sem=recv_sem.at[place, q],
             device_id={"exp": target},
             device_id_type=MESH,
@@ -410,7 +400,7 @@
         return pltpu.make_async_remote_copy(
             src_ref=last_out.at[q],
             dst_ref=last_in.at[q],
-            send_sem=last_send.at[q],
+            send_sem=last_send.at[0],
             recv_sem=last_recv.at[q],
             device_id={"exp": target},
             device_id_type=MESH,
@@ -449,7 +439,37 @@
                 moving[d, q] = value.astype(jnp.bfloat16)
                 part_copy(right, s, q).start()
 
-    per_turn = pl.cdiv(CHUNKS, n)
+    early, late = EARLY * STRIDE, (CHUNKS - EARLY) * STRIDE
+    events = early + late + (n - 1) * PARTS
+
+    def slot(t, carry):
+        for right in directions():
+            e = t - lag(right)
+            in_early = e < early
+            in_late = (e >= early + PARTS) & (e < early + PARTS + late)
+            of_depth = jnp.where(in_early, e, e - PARTS)
+            is_depth = (e >= 0) & (in_early | in_late)
+
+            @pl.when(is_depth & (lax.rem(of_depth, STRIDE) == 0))
+            def _(right=right, of_depth=of_depth):
+                c = of_depth // STRIDE
+
+                @pl.when(jnp.where(right, gets_raw_left, gets_raw_right))
+                def _():
+                    take_raw(c)
+
+                def one(s, carry):
+                    move_depth(right, s, c)
+                    return carry
+
+                lax.fori_loop(0, n - 1, one, 0)
+
+            @pl.when((e >= early) & (e < events) & jnp.logical_not(is_depth))
+            def _(right=right, e=e):
+                i = jnp.where(e < early + PARTS, e - early, e - early - late)
+                move_part(right, i // PARTS, lax.rem(i, PARTS))
+
+        return carry
 
     def turn(i, carry):
         correlate(pick(i))
@@ -462,30 +482,24 @@
             def _():
                 move_first(i - 1)
 
-        for k in range(per_turn):
-            depth_slot(i * per_turn + k)
+                @pl.when(i == 1)
+                def _():
+                    for c in range(EARLY, CHUNKS):
+                        raw_copy(c).start()
+
+        @pl.when((i < EARLY) & jnp.logical_not(at_end))
+        def _():
+            lax.fori_loop(i * STRIDE, (i + 1) * STRIDE, slot, 0)
+
         return carry
 
     lax.fori_loop(0, n, turn, 0)
+
+    @pl.when(jnp.logical_not(at_end))
+    def _():
+        lax.fori_loop(early, events + LAG * (n - 3), slot, 0)
+
     complete(me)
-
-    def late_slot(t, carry):
-        depth_slot(t)
-        return carry
-
-    lax.fori_loop(n * per_turn, CHUNKS + LAG * (n - 3), late_slot, 0)
-
-    def forward(t, carry):
-        for right in directions():
-            i = t - lag(right)
-
-            @pl.when((i >= 0) & (i < (n - 1) * PARTS))
-            def _(right=right, i=i):
-                move_part(right, i // PARTS, lax.rem(i, PARTS))
-
-        return carry
-
-    lax.fori_loop(0, (n - 1) * PARTS + LAG * (n - 3), forward, 0)
 
     def bottom(c, carry):
         chunk_rows = pl.ds(pl.multiple_of(c * span, span), span)
@@ -525,11 +539,17 @@
         return pltpu.make_async_remote_copy(
             src_ref=det_mine.at[part_rows(q)],
             dst_ref=det_theirs.at[j - 1, part_rows(q)],
-            send_sem=det_send.at[j - 1, q],
+            send_sem=det_send.at[j - 1],
             recv_sem=det_recv.at[j - 1, q],
             device_id={"band": lax.rem(band + j, bands)},
             device_id_type=MESH,
         )
+
+    def out_copy(k, q):
+        rows = part_rows(q)
+        if k == 0:
+            return pltpu.make_async_copy(coadd.at[rows], coadd_out.at[rows], out_sem.at[k])
+        return pltpu.make_async_copy(detection.at[rows], detection_out.at[rows], out_sem.at[k])
 
     def finish(q, carry):
         rows = part_rows(q)
@@ -549,6 +569,7 @@
 
         value = result[me, rows] / below[rows]
         coadd[rows] = value
+        out_copy(0, q).start()
         det_mine[rows] = value * value * below[rows]
         for j in range(1, bands):
             det_copy(j, q).start()
@@ -556,58 +577,47 @@
 
     lax.fori_loop(0, PARTS, finish, 0)
 
+    def sent(ref, sem):
+        pltpu.make_async_remote_copy(
+            src_ref=ref,
+            dst_ref=ref,
+            send_sem=sem,
+            recv_sem=sem,
+            device_id={"band": lax.rem(band + 1, bands)},
+            device_id_type=MESH,
+        ).wait_send()
+
     @pl.when(at_end)
     def _():
         table_copy().wait_send()
-
-        def drain_raw(c, carry):
-            raw_copy(c).wait_send()
-            return carry
-
-        lax.fori_loop(0, CHUNKS, drain_raw, 0)
-
-    @pl.when(jnp.logical_not(at_end))
-    def _():
-        def drain_depth(i, carry):
-            s, c = i // CHUNKS, lax.rem(i, CHUNKS)
-            for right in directions():
-
-                @pl.when(step(right, s)[1])
-                def _(right=right):
-                    depth_copy(right, s, c).wait_send()
-
-            return carry
-
-        lax.fori_loop(0, (n - 1) * CHUNKS, drain_depth, 0)
-
-    def drain(i, carry):
-        s, q = i // PARTS, lax.rem(i, PARTS)
+        sent(weights, raw_send.at[0])
+
+    def drain(s, carry):
         for right in directions():
+            d, sends, _gets, _place, _target = step(right, s)
             to_end = jnp.where(right, me == n - 2, me == 1) & (s == 0)
-            sends = step(right, s)[1]
+
+            @pl.when(sends & jnp.logical_not(at_end))
+            def _(d=d):
+                sent(depth_moving.at[d], depth_send.at[d])
 
             @pl.when(sends & to_end)
             def _():
-                last_copy(q).wait_send()
+                sent(last_out, last_send.at[0])
 
             @pl.when(sends & jnp.logical_not(to_end))
-            def _(right=right):
-                part_copy(right, s, q).wait_send()
-
-        return carry
-
-    lax.fori_loop(0, (n - 1) * PARTS, drain, 0)
-
-    def drain_spill(d, carry):
-        for side in range(2):
-
-            @pl.when(sends_spill[side])
-            def _(side=side):
-                spill_copy(side, d).wait_send()
-
-        return carry
-
-    lax.fori_loop(0, n, drain_spill, 0)
+            def _(d=d):
+                sent(moving.at[d], send_sem.at[d])
+
+        return carry
+
+    lax.fori_loop(0, n - 1, drain, 0)
+
+    for side in range(2):
+
+        @pl.when(sends_spill[side])
+        def _(side=side):
+            sent(spilling.at[side], spill_send.at[side])
 
     def combine(q, carry):
         rows = part_rows(q)
@@ -616,16 +626,15 @@
             det_copy(j, q).wait_recv()
             value += det_theirs[j - 1, rows]
         detection[rows] = value
+        out_copy(1, q).start()
         return carry
 
     lax.fori_loop(0, PARTS, combine, 0)
 
-    def drain_det(q, carry):
-        for j in range(1, bands):
-            det_copy(j, q).wait_send()
-        return carry
-
-    lax.fori_loop(0, PARTS, drain_det, 0)
+    for j in range(1, bands):
+        sent(det_mine, det_send.at[j - 1])
+    pltpu.make_async_copy(coadd, coadd_out, out_sem.at[0]).wait()
+    pltpu.make_async_copy(detection, detection_out, out_sem.at[1]).wait()
 
 
 def local(sizes, images, mask_bits, inv_var, routes, block_slot, kernel_index, coefficients):
@@ -646,6 +655,8 @@
     bf16, f32 = jnp.bfloat16, jnp.float32
     dma = pltpu.SemaphoreType.DMA
     scratch = [
+        pltpu.VMEM((tile_rows, tile_cols), f32),
+        pltpu.VMEM((tile_rows, tile_cols), f32),
         pltpu.VMEM(across.shape, bf16),
         pltpu.VMEM(down.shape, bf16),
         pltpu.VMEM((held, block, block), bf16),
@@ -671,19 +682,20 @@
         pltpu.VMEM((bands - 1, tile_rows, tile_cols), f32),
         dma((2,)),
         dma((CHUNKS, 2)),
-        dma((CHUNKS,)),
+        dma((1,)),
         dma((CHUNKS,)),
         dma((2,)),
-        dma((n, CHUNKS)),
+        dma((n,)),
         dma((n + 1, CHUNKS)),
-        dma((n, PARTS)),
+        dma((n,)),
         dma((n + 1, PARTS)),
+        dma((1,)),
         dma((PARTS,)),
-        dma((PARTS,)),
+        dma((2,)),
         dma((2, n)),
-        dma((2, n)),
+        dma((bands - 1,)),
         dma((bands - 1, PARTS)),
-        dma((bands - 1, PARTS)),
+        dma((2,)),
     ]
     held_bytes = sum(
         int(np.prod(x.shape)) * jnp.dtype(x.dtype).itemsize
@@ -695,7 +707,7 @@
         functools.partial(coadd_kernel, n, strips, bands),
         out_shape=(whole, whole),
         in_specs=[smem] * 5 + [anywhere] * 4,
-        out_specs=(vmem, vmem),
+        out_specs=(pl.BlockSpec(memory_space=pl.ANY),) * 2,
         scratch_shapes=scratch,
         compiler_params=pltpu.CompilerParams(collective_id=0, has_side_effects=True, vmem_limit_bytes=limit),
         name="coadd",

time: 41.9 us -> 41 us (0.979)
  Pallas kernels: 39.5 us -> 38.6 us
    pallas_call x1, Pallas kernels: 39.5 us -> 38.6 us  [local(): pl.pallas_call(functools.partial(coadd_kernel, n, strips, bands), out_sha...]
where the time goes in v4:
time: 41 us; the launch traced here: 40.9 us
  Pallas kernels  38.6 us (94%)
  local copies, waits for them, and re-layouts  1.59 us (4%)
  between operations  0.64 us (2%)
    pallas_call x1, Pallas kernels, local(): pl.pallas_call(functools.partial(coadd_kernel, n, strips, bands), out_sha...  38.6 us
    unnamed x2, local copies, waits for them, and re-layouts  1.59 us

profile of v4, /device:TPU:0, one launch (start us, length us, event | category | flops | bytes accessed | tf_op | source)
XLA Modules:
  0.0 40.9 jit_solution(12447181199556090329)
XLA Ops:
  0.6 38.6 %coadd.1 = (f32[256,512]{1,0:T(8,128)S(1)}, f32[256,512]{1,0:T(8,128)S(1)}) custom-call(s32[16]{0:T(128)} %bitcast.12, s32[16]{0:T(128)} %bitcast.13, s32[16]{0:T(128)} %bitcast.14, f32[16]{0:T(128)} %bitcast.15, f32[3,64]{1,0:T(4,128)} %bitcast.11, bf16[16,128,128]{2,1,0:T(8,128)(2,1)} %bitcast.10, s32[16,128,128]{2,1,0:T(8,128)} %bitcast.9, ...), custom_call_target="tpu_custom_call" | custom-call | tf_op jit(solution)/shard_map/coadd/pallas_call | solution.py:706
  39.3 0.8 %copy.13 = f32[1,256,512]{2,1,0:T(8,128)} copy(f32[1,256,512]{2,1,0:T(8,128)S(1)} %bitcast.8) | data formatting | bytes 1048576
  40.1 0.8 %copy.14 = f32[256,512]{1,0:T(8,128)} copy(f32[256,512]{1,0:T(8,128)S(1)} %get-tuple-element.9) | data formatting | bytes 1048576

commit v5 on v4

--- a/solution.py
+++ b/solution.py
@@ -17,6 +17,7 @@
 PARTS = 8
 STRIDE = 4
 EARLY = 3
+WIDE = 4
 LAG = 6
 
 kernel_sigmas = (1.0, 2.5, 6.0)
@@ -422,19 +423,19 @@
 
     def move_part(right, s, q):
         d, sends, _gets, _place, _target = step(right, s)
-        to_end = jnp.where(right, me == n - 2, me == 1) & (s == 0)
+        wide = jnp.where(right, me == n - 2, me == 1) & (s == 0) & (q < WIDE)
 
         @pl.when(sends & jnp.logical_not(at_end))
         def _():
             arrived(moving, recv_sem, d, q)
             value = moving[d, q].astype(jnp.float32) + result[d, part_rows(q)]
 
-            @pl.when(to_end)
+            @pl.when(wide)
             def _():
                 last_out[q] = value
                 last_copy(q).start()
 
-            @pl.when(jnp.logical_not(to_end))
+            @pl.when(jnp.logical_not(wide))
             def _():
                 moving[d, q] = value.astype(jnp.bfloat16)
                 part_copy(right, s, q).start()
@@ -554,10 +555,16 @@
     def finish(q, carry):
         rows = part_rows(q)
 
-        @pl.when(at_end)
+        @pl.when(at_end & (q < WIDE))
         def _():
             last_copy(q).wait_recv()
             result[me, rows] += last_in[q]
+
+        @pl.when(at_end & (q >= WIDE))
+        def _():
+            place = jnp.where(at_left, n, me)
+            arrived(moving, recv_sem, place, q)
+            result[me, rows] += moving[place, q].astype(jnp.float32)
 
         @pl.when(jnp.logical_not(at_end))
         def _():
@@ -602,8 +609,9 @@
                 sent(depth_moving.at[d], depth_send.at[d])
 
             @pl.when(sends & to_end)
-            def _():
+            def _(d=d):
                 sent(last_out, last_send.at[0])
+                sent(moving.at[d, pl.ds(WIDE, PARTS - WIDE)], send_sem.at[d])
 
             @pl.when(sends & jnp.logical_not(to_end))
             def _(d=d):
@@ -673,8 +681,8 @@
         pltpu.VMEM((n, tile_rows, tile_cols), f32),
         pltpu.VMEM((n + 1, CHUNKS, BLOCK_ROWS, span, tile_cols), bf16),
         pltpu.VMEM((n + 1, PARTS, part, tile_cols), bf16),
-        pltpu.VMEM((PARTS, part, tile_cols), f32),
-        pltpu.VMEM((PARTS, part, tile_cols), f32),
+        pltpu.VMEM((WIDE, part, tile_cols), f32),
+        pltpu.VMEM((WIDE, part, tile_cols), f32),
         pltpu.VMEM((2, n, SPILL, tile_cols), bf16),
         pltpu.VMEM((2, n, SPILL, tile_cols), bf16),
         pltpu.VMEM((tile_rows, tile_cols), f32),
@@ -690,7 +698,7 @@
         dma((n,)),
         dma((n + 1, PARTS)),
         dma((1,)),
-        dma((PARTS,)),
+        dma((WIDE,)),
         dma((2,)),
         dma((2, n)),
         dma((bands - 1,)),

time: 41 us -> 38.3 us (0.934)
  Pallas kernels: 38.6 us -> 35.9 us
    pallas_call x1, Pallas kernels: 38.6 us -> 35.9 us  [local(): pl.pallas_call(functools.partial(coadd_kernel, n, strips, bands), out_sha...]
where the time goes in v5:
time: 38.3 us; the launch traced here: 38.1 us
  Pallas kernels  35.9 us (94%)
  local copies, waits for them, and re-layouts  1.59 us (4%)
  between operations  0.64 us (2%)
    pallas_call x1, Pallas kernels, local(): pl.pallas_call(functools.partial(coadd_kernel, n, strips, bands), out_sha...  35.9 us
    unnamed x2, local copies, waits for them, and re-layouts  1.59 us

profile of v5, /device:TPU:0, one launch (start us, length us, event | category | flops | bytes accessed | tf_op | source)
XLA Modules:
  0.0 38.1 jit_solution(4855139962403145144)
XLA Ops:
  0.6 35.9 %coadd.1 = (f32[256,512]{1,0:T(8,128)S(1)}, f32[256,512]{1,0:T(8,128)S(1)}) custom-call(s32[16]{0:T(128)} %bitcast.12, s32[16]{0:T(128)} %bitcast.13, s32[16]{0:T(128)} %bitcast.14, f32[16]{0:T(128)} %bitcast.15, f32[3,64]{1,0:T(4,128)} %bitcast.11, bf16[16,128,128]{2,1,0:T(8,128)(2,1)} %bitcast.10, s32[16,128,128]{2,1,0:T(8,128)} %bitcast.9, ...), custom_call_target="tpu_custom_call" | custom-call | tf_op jit(solution)/shard_map/coadd/pallas_call | solution.py:714
  36.5 0.8 %copy.13 = f32[1,256,512]{2,1,0:T(8,128)} copy(f32[1,256,512]{2,1,0:T(8,128)S(1)} %bitcast.8) | data formatting | bytes 1048576
  37.3 0.8 %copy.14 = f32[256,512]{1,0:T(8,128)} copy(f32[256,512]{1,0:T(8,128)S(1)} %get-tuple-element.9) | data formatting | bytes 1048576

commit v6 on v5

--- a/solution.py
+++ b/solution.py
@@ -17,7 +17,8 @@
 PARTS = 8
 STRIDE = 4
 EARLY = 3
-WIDE = 4
+WIDE = 3
+HANDS = 1
 LAG = 6
 
 kernel_sigmas = (1.0, 2.5, 6.0)
@@ -643,6 +644,19 @@
         sent(det_mine, det_send.at[j - 1])
     pltpu.make_async_copy(coadd, coadd_out, out_sem.at[0]).wait()
     pltpu.make_async_copy(detection, detection_out, out_sem.at[1]).wait()
+
+
+def hand_out_kernel(coadd, detection, coadd_out, detection_out, sem):
+    rows = coadd.shape[0] // HANDS
+    copies = []
+    for q in range(HANDS):
+        part = pl.ds(q * rows, rows)
+        for k, (src, dst) in enumerate(((coadd, coadd_out), (detection, detection_out))):
+            copies.append(pltpu.make_async_copy(src.at[part], dst.at[part], sem.at[k, q]))
+    for copy in copies:
+        copy.start()
+    for copy in copies:
+        copy.wait()
 
 
 def local(sizes, images, mask_bits, inv_var, routes, block_slot, kernel_index, coefficients):
@@ -726,6 +740,15 @@
             coefficients.T, images[0, 0], mask_bits[0, 0], across, down,
         )
     ])
+    coadd, detection = pl.pallas_call(
+        hand_out_kernel,
+        out_shape=(whole, whole),
+        in_specs=[pl.BlockSpec(memory_space=pl.ANY)] * 2,
+        out_specs=(anywhere,) * 2,
+        scratch_shapes=[dma((2, HANDS))],
+        compiler_params=pltpu.CompilerParams(vmem_limit_bytes=1 << 20),
+        name="hand_out",
+    )(coadd, detection)
     return coadd[None], detection
 
 

time: 38.3 us -> 37.4 us (0.977)
  local copies, waits for them, and re-layouts: 1.59 us -> 0 us
  Pallas kernels: 35.9 us -> 36.6 us
    unnamed x2 -> x0, local copies, waits for them, and re-layouts: 1.59 us -> none
    pallas_call x0 -> x1, Pallas kernels: none -> 0.99 us  [local(): pl.pallas_call(hand_out_kernel, out_shape=(whole, whole), in_specs=[pl.Bl...]
where the time goes in v6:
time: 37.4 us; the launch traced here: 37.2 us
  Pallas kernels  36.6 us (98%)
  between operations  0.64 us (2%)
    pallas_call x1, Pallas kernels, local(): pl.pallas_call(functools.partial(coadd_kernel, n, strips, bands), out_sha...  35.6 us
    pallas_call x1, Pallas kernels, local(): pl.pallas_call(hand_out_kernel, out_shape=(whole, whole), in_specs=[pl.Bl...  0.99 us

profile of v6, /device:TPU:0, one launch (start us, length us, event | category | flops | bytes accessed | tf_op | source)
XLA Modules:
  0.0 37.2 jit_solution(1484372600457031277)
XLA Ops:
  0.6 35.6 %coadd.1 = (f32[256,512]{1,0:T(8,128)S(1)}, f32[256,512]{1,0:T(8,128)S(1)}) custom-call(s32[16]{0:T(128)} %bitcast.11, s32[16]{0:T(128)} %bitcast.12, s32[16]{0:T(128)} %bitcast.13, f32[16]{0:T(128)} %bitcast.14, f32[3,64]{1,0:T(4,128)} %bitcast.10, bf16[16,128,128]{2,1,0:T(8,128)(2,1)} %bitcast.9, s32[16,128,128]{2,1,0:T(8,128)} %bitcast.8, ...), custom_call_target="tpu_custom_call" | custom-call | tf_op jit(solution)/shard_map/coadd/pallas_call | solution.py:728
  36.2 1.0 %hand_out.1 = (f32[256,512]{1,0:T(8,128)}, f32[256,512]{1,0:T(8,128)}) custom-call(f32[256,512]{1,0:T(8,128)S(1)} %get-tuple-element.6.coadd, f32[256,512]{1,0:T(8,128)S(1)} %get-tuple-element.7.detection), custom_call_target="tpu_custom_call" | custom-call | tf_op jit(solution)/shard_map/hand_out/pallas_call | solution.py:743
